TPU v7x, 32 devices: a whole 2x2x4 slice. The times are simulated.
32 devices in a mesh: grp: 2 (over y), frm: 4 (over z), row: 4 (over x, core).
Axes of the slice: x: 2, y: 2, z: 4, core: 2. Of those that a mesh axis runs over, the one named last changes fastest.
Arguments:
- queries: bfloat16 [16, 8, 128, 2240], P(('grp', 'frm'), 'row'), parts along dimension 0, may hold values from -6 to 6
- keys: bfloat16 [16, 8, 128, 2240], P(('grp', 'frm'), 'row'), parts along dimension 0, may hold values from -6 to 6
- values: bfloat16 [16, 8, 128, 2240], P(('grp', 'frm'), 'row'), parts along dimension 0, may hold values from -6 to 6
- flags: int32 [16], P(('grp', 'frm')), parts along dimension 0, may hold values 0 or 1
- blocks: int32 [16], P(('grp', 'frm')), parts along dimension 0, may hold values from 0 to 2, as said below
- out_weight: bfloat16 [2240, 2240], P('frm'), may hold values from -0.125 to 0.125
- norm_gain: float32 [2240], replicated, may hold values from 0.1 to 1.9
Outputs:
- projected: bfloat16 [16, 8, 128, 2240], P(('grp', 'frm'), 'row'), parts along dimension 0
There are 2 independent parts, one for each index of `grp`. A program takes and returns all parts, laid end to end along the dimension named above; an argument that names none is the same for every part. Nothing has to cross between parts.
Inputs may be any that keep to these rules, and one draw needn't show every extreme that they name: `flags`: 1 marks a clean frame, 0 a noisy one. `blocks`: within the 8 frames of one group, block numbers never fall and each block is 1 to 4 consecutive frames, some block exactly 4; every number from 0 to 2 occurs.
All inputs are finite; a program needn't handle non-finite values. No bound on the sum of `flags` on one device may be relied on, other than what follows from the above.
Results may differ from a plain program's by a relative error of at most 0.0049.
Values may be sent and summed in bfloat16 or wider, within the bound.
No kernel may reach another device: no remote copies, remote signals or barrier semaphores. Data moves between devices by JAX's collectives and lax.ppermute only.
A program may use at most 192 MiB of HBM per device.

v0:
```python
import jax
import jax.numpy as jnp
from jax import lax
from jax.sharding import PartitionSpec as P

HEADS = 20
HD = 112
norm_eps = 1e-06


def entering(part, axis, combine, identity):
    place = lax.axis_index(axis)
    gathered = jax.tree.map(lambda a: lax.all_gather(a, axis), part)
    state = jax.tree.map(lambda a, e: jnp.zeros_like(a) + jnp.asarray(e, a.dtype), part, identity)

    def one(step, state):
        return combine(
            state, jax.tree.map(lambda a: lax.dynamic_index_in_dim(a, step, 0, False), gathered)
        )

    return lax.fori_loop(0, place, one, state)


def combine(earlier, later):
    closed_a, opened_a, latest_a = earlier
    closed_b, opened_b, latest_b = later
    advance = (latest_a < latest_b).astype(jnp.float32)
    return (
        closed_a + closed_b + advance * opened_a,
        opened_b + (1.0 - advance) * opened_a,
        jnp.maximum(latest_a, latest_b),
    )


def empty_carry(length):
    return (
        jnp.zeros((length,), jnp.float32),
        jnp.zeros((length,), jnp.float32),
        jnp.full((1,), -1.0, jnp.float32),
    )


def frame_element(frame_states, flag_values, block_values, frame_idx):
    length = frame_states.shape[1]
    return (
        jnp.zeros((length,), jnp.float32),
        flag_values[frame_idx] * frame_states[frame_idx],
        block_values[frame_idx : frame_idx + 1],
    )


def fold_frames(frame_states, flag_values, block_values):
    running = empty_carry(frame_states.shape[1])
    for frame_idx in range(frame_states.shape[0]):
        running = combine(
            running, frame_element(frame_states, flag_values, block_values, frame_idx)
        )
    return running


def read_frames(prefix, frame_states, flag_values, block_values):
    running = prefix
    collected = []
    for frame_idx in range(frame_states.shape[0]):
        advance = (running[2] < block_values[frame_idx : frame_idx + 1]).astype(jnp.float32)
        select = jnp.maximum(advance, flag_values[frame_idx])
        collected.append(running[0] + select * running[1] + frame_states[frame_idx])
        running = combine(
            running, frame_element(frame_states, flag_values, block_values, frame_idx)
        )
    return jnp.stack(collected)


def local(queries, keys, values, flags, blocks, out_weight, norm_gain):
    frames, lat_rows, lat_cols, model_width = queries.shape
    tokens = lat_rows * lat_cols
    key_pos = jax.nn.relu(keys).reshape(frames, tokens, HEADS, HD)
    value_heads = values.reshape(frames, tokens, HEADS, HD)
    partial_value = jnp.einsum(
        "ftha,fthb->fhab", key_pos, value_heads, preferred_element_type=jnp.float32
    )
    partial_value = partial_value.reshape(frames, HEADS * HD * HD)
    flag_values = flags.astype(jnp.float32)
    block_values = blocks.astype(jnp.float32)
    summed = lax.psum(partial_value, "row")
    totals = fold_frames(summed, flag_values, block_values)
    prefix = entering(
        (totals[0], totals[1], totals[2]), "frm", combine, empty_carry(summed.shape[1])
    )
    read_states = read_frames(prefix, summed, flag_values, block_values)
    read_tensor = read_states.reshape(frames, HEADS, HD, HD)
    query_pos = jax.nn.relu(queries).reshape(frames, tokens, HEADS, HD).astype(jnp.float32)
    attended = jnp.einsum(
        "ftha,fhab->fthb", query_pos, read_tensor, precision=lax.Precision.HIGHEST
    )
    inv_rms = lax.rsqrt(jnp.mean(attended * attended, axis=-1, keepdims=True) + norm_eps)
    gain_table = norm_gain.reshape(HEADS, HD)
    normed = (
        (attended * inv_rms * gain_table).astype(jnp.bfloat16).reshape(frames * tokens, model_width)
    )
    projected = jnp.dot(
        normed,
        lax.all_gather(out_weight, "frm", axis=0, tiled=True),
        preferred_element_type=jnp.float32,
    )
    return projected.astype(jnp.bfloat16).reshape(frames, lat_rows, lat_cols, model_width)


def solution(mesh):
    in_specs = (
        P(("grp", "frm"), "row", None, None),
        P(("grp", "frm"), "row", None, None),
        P(("grp", "frm"), "row", None, None),
        P(("grp", "frm")),
        P(("grp", "frm")),
        P("frm", None),
        P(),
    )
    out_specs = P(("grp", "frm"), "row", None, None)
    return jax.shard_map(local, mesh=mesh, in_specs=in_specs, out_specs=out_specs, check_vma=False)
```

profile of v0, /device:TPU:0, one launch (start us, length us, event | category | flops | bytes accessed | tf_op | source)
XLA Modules:
  0.0 476.6 jit_solution(3732474962754750551)
XLA Ops:
  8.3 10.3 %copy.16 = bf16[2,2,128,2240]{2,1,3,0:T(2,128)(2,1)} copy(bf16[2,2,128,2240]{2,3,1,0:T(8,128)(2,1)S(1)} %broadcast_maximum_fusion.1) | data formatting | bytes 4587520 | tf_op jit(solution)/shard_map/jit(relu)/max | solution.py:77
  18.7 5.2 %reshape.37 = bf16[2,256,20,112]{1,3,2,0:T(8,128)(2,1)S(1)} reshape(bf16[2,2,128,2240]{2,1,3,0:T(2,128)(2,1)} %copy.16) | data formatting | bytes 4587520 | tf_op jit(solution)/shard_map/reshape | solution.py:77
  23.9 12.6 %copy.17 = bf16[2,2,128,2240]{2,1,3,0:T(2,128)(2,1)} copy(bf16[2,2,128,2240]{2,3,1,0:T(8,128)(2,1)} %param.11) | data formatting | bytes 4587520 | tf_op args[2]
  36.5 6.2 %reshape.38 = bf16[2,256,20,112]{1,3,2,0:T(8,128)(2,1)} reshape(bf16[2,2,128,2240]{2,1,3,0:T(2,128)(2,1)} %copy.17) | data formatting | bytes 4587520 | tf_op jit(solution)/shard_map/reshape | solution.py:78
  42.7 3.8 fusion.10
  46.5 5.6 %reshape.39 = f32[2,250880]{1,0:T(2,128)} reshape(f32[2,20,112,112]{3,2,1,0:T(8,128)} %fusion.10) | data formatting | bytes 4014080 | tf_op jit(solution)/shard_map/reshape | solution.py:82
  56.6 48.6 %all-reduce.3.cloned.1.call-done = f32[2,250880]{1,0:T(2,128)} async-done(((f32[2,250880]{1,0:T(2,128)}), f32[2,250880]{1,0:T(2,128)}) %all-reduce.3.cloned.1.call-update) | async-done | bytes 2007056 | tf_op jit(solution)/shard_map/psum | solution.py:85
  105.1 8.0 %fusion.8 = (f32[1,250880]{1,0:T(1,128)S(1)}, f32[1,1,250880]{2,1,0:T(1,128)}, f32[1,1,250880]{2,1,0:T(1,128)}, f32[1,250880]{1,0:T(1,128)}) fusion(f32[2,250880]{1,0:T(2,128)} %all-reduce.3.cloned.1.call-done, f32[]{:T(128)} %bitcast.7, f32[]{:T(128)} %bitcast.6, f32[]{:T(128)} %bitcast.5, f32[]{:T(128)} %bitcast.12, f32[]{:T(128)} %bitcast.11), kind=kLoop, calls=%fused_computation.27 | loop fusion | flops 1505280 | bytes 6021140 | tf_op jit(solution)/shard_map/slice | solution.py:47
  114.4 11.9 %all-reduce = f32[4]{0:T(128)S(1)} all-reduce(f32[4]{0:T(128)S(1)} %get-tuple-element.81), channel_id=2, replica_groups=mesh['grp'=2,'frm'=4,'row'=4] {'frm'}, use_global_device_ids=true, to_apply=%add | all-reduce | flops 4 | bytes 32
  126.4 10.1 %copy.20 = bf16[2,2,128,2240]{2,1,3,0:T(2,128)(2,1)S(1)} copy(bf16[2,2,128,2240]{2,3,1,0:T(8,128)(2,1)S(1)} %broadcast_maximum_fusion) | data formatting | bytes 4587520 | tf_op jit(solution)/shard_map/jit(relu)/max | solution.py:92
  136.5 2.7 reshape.40
  139.3 51.7 %all-gather.11.cloned.1.call-done = f32[4,1,250880]{2,1,0:T(1,128)} async-done(((f32[1,1,250880]{2,1,0:T(1,128)}), f32[4,1,250880]{2,1,0:T(1,128)}) %all-gather.11.cloned.1.call-update) | async-done | bytes 4014096 | tf_op jit(solution)/shard_map/all_gather | solution.py:13
  191.1 5.5 %copy.28 = f32[4,1,250880]{2,0,1:T(4,128)} copy(f32[4,1,250880]{2,1,0:T(1,128)} %all-gather.11.cloned.1.call-done) | data formatting | bytes 8028160
  196.5 72.4 %all-gather.9.cloned.1.call-done = f32[4,1,250880]{2,1,0:T(1,128)} async-done(((f32[1,1,250880]{2,1,0:T(1,128)}), f32[4,1,250880]{2,1,0:T(1,128)}) %all-gather.9.cloned.1.call-update) | async-done | bytes 4014096 | tf_op jit(solution)/shard_map/all_gather | solution.py:13
  268.9 5.5 %copy.29 = f32[4,1,250880]{2,0,1:T(4,128)} copy(f32[4,1,250880]{2,1,0:T(1,128)} %all-gather.9.cloned.1.call-done) | data formatting | bytes 8028160
  277.9 3.6 add_add_fusion.1
  281.5 1.9 stack.9
  283.8 3.0 stack.10
  286.7 2.7 copy.19
  289.4 3.7 fusion
  293.9 2.4 copy.21
  296.7 153.4 %all-gather.7.cloned.1.call-done = bf16[2240,2240]{1,0:T(8,128)(2,1)} async-done(((bf16[560,2240]{1,0:T(8,128)(2,1)}), bf16[2240,2240]{1,0:T(8,128)(2,1)}) %all-gather.7.cloned.1.call-update) | async-done | bytes 10035216 | tf_op jit(solution)/shard_map/all_gather | solution.py:103
  450.1 13.4 %convolution_convert_fusion = bf16[512,2240]{0,1:T(8,128)(2,1)} fusion(bf16[512,2240]{0,1:T(8,128)(2,1)S(1)} %bitcast.74, bf16[2240,2240]{1,0:T(8,128)(2,1)} %all-gather.7.cloned.1.call-done), kind=kOutput, calls=%fused_computation.10 | convolution fusion | flops 5139169280 | bytes 14622720 | tf_op jit(solution)/shard_map/dot_general | solution.py:101
  463.6 4.8 %reshape.42 = bf16[2,2,128,2240]{2,1,0,3:T(2,128)(2,1)S(1)} reshape(bf16[512,2240]{0,1:T(8,128)(2,1)} %convolution_convert_fusion) | data formatting | bytes 4587520 | tf_op jit(solution)/shard_map/reshape | solution.py:106
  (37 shorter events, 9.5 us)
Async XLA Ops:
  6.5 98.6 %all-reduce.3.cloned.1.call-start = ((), (), s32[]{:S(2)}) async-start(), calls=%async_computation | async-start | bytes 4014080 | tf_op jit(solution)/shard_map/psum | solution.py:85
  46.5 5.6 %copy-start.3 = (s32[2]{0:T(128)S(1)}, s32[2]{0:T(128)}, u32[]{:S(2)}) copy-start(s32[2]{0:T(128)} %param.13) | copy-start | bytes 28
  46.5 5.7 %copy-start.5 = (u32[32]{0:T(128)S(1)}, u32[32]{0:T(128)}, u32[]{:S(2)}) copy-start(u32[32]{0:T(128)} %constant.52) | copy-start | bytes 388
  46.5 9.4 %copy-start.4 = (s32[2]{0:T(128)S(1)}, s32[2]{0:T(128)}, u32[]{:S(2)}) copy-start(s32[2]{0:T(128)} %param.12) | copy-start | bytes 28
  52.0 139.0 %all-gather.11.cloned.1.call-start = ((), (), s32[]{:S(2)}) async-start(), calls=%async_computation.3 | async-start | bytes 5017600 | tf_op jit(solution)/shard_map/all_gather | solution.py:13
  113.1 13.2 %copy-start.1 = (bf16[2,2,128,2240]{2,3,1,0:T(8,128)(2,1)S(1)}, bf16[2,2,128,2240]{2,3,1,0:T(8,128)(2,1)}, u32[]{:S(2)}) copy-start(bf16[2,2,128,2240]{2,3,1,0:T(8,128)(2,1)} %param.9) | copy-start | bytes 6881284
  113.1 155.8 %all-gather.9.cloned.1.call-start = ((), (), s32[]{:S(2)}) async-start(), calls=%async_computation.2 | async-start | bytes 5017600 | tf_op jit(solution)/shard_map/all_gather | solution.py:13
  113.8 336.3 %all-gather.7.cloned.1.call-start = ((), (), s32[]{:S(2)}) async-start(), calls=%async_computation.1 | async-start | bytes 12902400 | tf_op jit(solution)/shard_map/all_gather | solution.py:103
  136.5 2.8 copy-start.2
  283.8 5.7 %copy-start = (bf16[2,256,20,112]{1,3,2,0:T(8,128)(2,1)S(1)}, bf16[2,256,20,112]{1,3,2,0:T(8,128)(2,1)}, u32[]{:S(2)}) copy-start(bf16[2,256,20,112]{1,3,2,0:T(8,128)(2,1)} %reshape.40) | copy-start | bytes 6881284
Sparse Core Ops, SparseCore 0:
  52.2 52.9 all-reduce.2
  113.2 77.8 all-gather.10
  192.6 76.2 all-gather.8
  270.3 179.7 all-gather.6
where the time goes:
time: 477 us
  waiting for transfers between devices  327 us (69%)
  local copies, waits for them, and re-layouts  82.4 us (17%)
  matrix products  21 us (4%)
  between operations  18.3 us (4%)
  other arithmetic  15.5 us (3%)
  blocking collectives  11.9 us (2%)
    all_gather x1, waiting for transfers between devices, local(): lax.all_gather(out_weight, 'frm', axis=0, tiled=True)  153 us
    all_gather x2, waiting for transfers between devices, entering(): gathered = jax.tree.map(lambda a: lax.all_gather(a, axis), part)  124 us
    psum x1, waiting for transfers between devices, local(): summed = lax.psum(partial_value, 'row')  48.6 us
    unnamed x18, local copies, waits for them, and re-layouts  24.6 us
    dot_general x1, matrix products, local(): jnp.dot(normed, lax.all_gather(out_weight, 'frm', axis=0, tiled=True), pr...  13.4 us
    unnamed x1, blocking collectives  11.9 us
    max x1, local copies, waits for them, and re-layouts, local(): key_pos = jax.nn.relu(keys).reshape(frames, tokens, HEADS, HD)  10.3 us
    max x1, local copies, waits for them, and re-layouts, local(): jax.nn.relu(queries).reshape(frames, tokens, HEADS, HD).astype(jnp.float32)  10.1 us
  transfers between devices with their start and end apart: 4, of which 4 were waited for; matrix products, arithmetic and copies ran while one was open for 10% of the time, Pallas kernels for 0%

commit v1 on v0

--- a/solution.py
+++ b/solution.py
@@ -82,7 +82,7 @@
     partial_value = partial_value.reshape(frames, HEADS * HD * HD)
     flag_values = flags.astype(jnp.float32)
     block_values = blocks.astype(jnp.float32)
-    summed = lax.psum(partial_value, "row")
+    summed = lax.all_gather(partial_value, axis_name="row").sum(axis=0)
     totals = fold_frames(summed, flag_values, block_values)
     prefix = entering(
         (totals[0], totals[1], totals[2]), "frm", combine, empty_carry(summed.shape[1])

time: 477 us -> 490 us (1.027)
  waiting for transfers between devices: 327 us -> 333 us
  other arithmetic: 15.5 us -> 21.3 us
    all_gather x0 -> x1, waiting for transfers between devices: none -> 54.6 us  [local(): summed = lax.all_gather(partial_value, axis_name='row').sum(axis=0)]
    psum x1 -> x0, waiting for transfers between devices: 48.6 us -> none  [local(): summed = lax.psum(partial_value, 'row')]
    reduce_sum x0 -> x1, other arithmetic: none -> 7.94 us  [local(): summed = lax.all_gather(partial_value, axis_name='row').sum(axis=0)]
    another operation x2 -> x3, local copies, waits for them, and re-layouts: 0.13 us -> 5.78 us  [the longest x1 5.64 us: local(): summed = lax.all_gather(partial_value, axis_name='row').sum(axis=0)]
    reshape x1 -> x0, local copies, waits for them, and re-layouts: 5.55 us -> none  [local(): partial_value = partial_value.reshape(frames, HEADS * HD * HD)]
  transfers between devices with their start and end apart: 4 -> 4, of which waited for: 4 -> 4; matrix products, arithmetic and copies ran while one was open for 10% -> 9% of each run, Pallas kernels for 0% -> 0%
where the time goes in v1:
time: 490 us; the launch traced here: 489 us
  waiting for transfers between devices  333 us (68%)
  local copies, waits for them, and re-layouts  82.5 us (17%)
  other arithmetic  21.3 us (4%)
  matrix products  21 us (4%)
  between operations  18.3 us (4%)
  blocking collectives  11.9 us (2%)
    all_gather x1, waiting for transfers between devices, local(): lax.all_gather(out_weight, 'frm', axis=0, tiled=True)  153 us
    all_gather x2, waiting for transfers between devices, entering(): gathered = jax.tree.map(lambda a: lax.all_gather(a, axis), part)  124 us
    all_gather x1, waiting for transfers between devices, local(): summed = lax.all_gather(partial_value, axis_name='row').sum(axis=0)  54.6 us
    unnamed x18, local copies, waits for them, and re-layouts  24.6 us
    dot_general x1, matrix products, local(): jnp.dot(normed, lax.all_gather(out_weight, 'frm', axis=0, tiled=True), pr...  13.4 us
    unnamed x1, blocking collectives  11.9 us
    max x1, local copies, waits for them, and re-layouts, local(): key_pos = jax.nn.relu(keys).reshape(frames, tokens, HEADS, HD)  10.3 us
    max x1, local copies, waits for them, and re-layouts, local(): jax.nn.relu(queries).reshape(frames, tokens, HEADS, HD).astype(jnp.float32)  10.1 us
  transfers between devices with their start and end apart: 4, of which 4 were waited for; matrix products, arithmetic and copies ran while one was open for 9% of the time, Pallas kernels for 0%

profile of v1, /device:TPU:0, one launch (start us, length us, event | category | flops | bytes accessed | tf_op | source)
XLA Modules:
  0.0 488.6 jit_solution(7940514945706562120)
XLA Ops:
  8.3 10.3 %copy.16 = bf16[2,2,128,2240]{2,1,3,0:T(2,128)(2,1)} copy(bf16[2,2,128,2240]{2,3,1,0:T(8,128)(2,1)S(1)} %broadcast_maximum_fusion.1) | data formatting | bytes 4587520 | tf_op jit(solution)/shard_map/jit(relu)/max | solution.py:77
  18.7 5.2 %reshape.34 = bf16[2,256,20,112]{1,3,2,0:T(8,128)(2,1)S(1)} reshape(bf16[2,2,128,2240]{2,1,3,0:T(2,128)(2,1)} %copy.16) | data formatting | bytes 4587520 | tf_op jit(solution)/shard_map/reshape | solution.py:77
  23.9 12.6 %copy.17 = bf16[2,2,128,2240]{2,1,3,0:T(2,128)(2,1)} copy(bf16[2,2,128,2240]{2,3,1,0:T(8,128)(2,1)} %param.11) | data formatting | bytes 4587520 | tf_op args[2]
  36.5 6.2 %reshape.35 = bf16[2,256,20,112]{1,3,2,0:T(8,128)(2,1)} reshape(bf16[2,2,128,2240]{2,1,3,0:T(2,128)(2,1)} %copy.17) | data formatting | bytes 4587520 | tf_op jit(solution)/shard_map/reshape | solution.py:78
  42.7 3.8 fusion.10
  46.5 5.6 %all_gather_reshape.3 = f32[1,2,250880]{2,1,0:T(2,128)} reshape(f32[2,20,112,112]{3,2,1,0:T(8,128)} %fusion.10) | data formatting | bytes 4014080 | tf_op jit(solution)/shard_map/all_gather;reshape | solution.py:85
  56.6 54.6 %all-gather.8.cloned.1.call-done = f32[4,2,250880]{2,1,0:T(2,128)} async-done(((f32[1,2,250880]{2,1,0:T(2,128)}), f32[4,2,250880]{2,1,0:T(2,128)}) %all-gather.8.cloned.1.call-update) | async-done | bytes 8028176 | tf_op jit(solution)/shard_map/all_gather | solution.py:85
  111.2 7.9 %reduce_sum.18 = f32[2,250880]{1,0:T(2,128)S(1)} reduce(f32[4,2,250880]{2,1,0:T(2,128)} %all-gather.8.cloned.1.call-done, f32[]{:T(128)} %constant.35.clone.1), dimensions={0}, to_apply=%region_0.1 | reduce | flops 1505280 | bytes 10035204 | tf_op jit(solution)/shard_map/reduce_sum | solution.py:85
  119.2 5.9 %fusion.8 = (f32[1,250880]{1,0:T(1,128)S(1)}, f32[1,1,250880]{2,1,0:T(1,128)}, f32[1,1,250880]{2,1,0:T(1,128)}, f32[1,250880]{1,0:T(1,128)}) fusion(f32[2,250880]{1,0:T(2,128)S(1)} %reduce_sum.18, f32[]{:T(128)} %bitcast.7, f32[]{:T(128)} %bitcast.6, f32[]{:T(128)} %bitcast.5, f32[]{:T(128)} %bitcast.12, f32[]{:T(128)} %bitcast.11), kind=kLoop, calls=%fused_computation.27 | loop fusion | flops 1505280 | bytes 6021140 | tf_op jit(solution)/shard_map/slice | solution.py:47
  126.4 11.9 %all-reduce = f32[4]{0:T(128)S(1)} all-reduce(f32[4]{0:T(128)S(1)} %get-tuple-element.81), channel_id=2, replica_groups=mesh['grp'=2,'frm'=4,'row'=4] {'frm'}, use_global_device_ids=true, to_apply=%add | all-reduce | flops 4 | bytes 32
  138.4 10.1 %copy.20 = bf16[2,2,128,2240]{2,1,3,0:T(2,128)(2,1)S(1)} copy(bf16[2,2,128,2240]{2,3,1,0:T(8,128)(2,1)S(1)} %broadcast_maximum_fusion) | data formatting | bytes 4587520 | tf_op jit(solution)/shard_map/jit(relu)/max | solution.py:92
  148.5 2.7 reshape.36
  151.3 51.7 %all-gather.14.cloned.1.call-done = f32[4,1,250880]{2,1,0:T(1,128)} async-done(((f32[1,1,250880]{2,1,0:T(1,128)}), f32[4,1,250880]{2,1,0:T(1,128)}) %all-gather.14.cloned.1.call-update) | async-done | bytes 4014096 | tf_op jit(solution)/shard_map/all_gather | solution.py:13
  203.0 5.5 %copy.28 = f32[4,1,250880]{2,0,1:T(4,128)} copy(f32[4,1,250880]{2,1,0:T(1,128)} %all-gather.14.cloned.1.call-done) | data formatting | bytes 8028160
  208.5 72.4 %all-gather.12.cloned.1.call-done = f32[4,1,250880]{2,1,0:T(1,128)} async-done(((f32[1,1,250880]{2,1,0:T(1,128)}), f32[4,1,250880]{2,1,0:T(1,128)}) %all-gather.12.cloned.1.call-update) | async-done | bytes 4014096 | tf_op jit(solution)/shard_map/all_gather | solution.py:13
  280.9 5.5 %copy.29 = f32[4,1,250880]{2,0,1:T(4,128)} copy(f32[4,1,250880]{2,1,0:T(1,128)} %all-gather.12.cloned.1.call-done) | data formatting | bytes 8028160
  289.9 3.6 add_add_fusion.1
  295.7 3.0 stack.10
  298.7 2.7 copy.19
  301.4 3.7 fusion
  305.8 2.4 copy.21
  308.7 153.4 %all-gather.10.cloned.1.call-done = bf16[2240,2240]{1,0:T(8,128)(2,1)} async-done(((bf16[560,2240]{1,0:T(8,128)(2,1)}), bf16[2240,2240]{1,0:T(8,128)(2,1)}) %all-gather.10.cloned.1.call-update) | async-done | bytes 10035216 | tf_op jit(solution)/shard_map/all_gather | solution.py:103
  462.1 13.4 %convolution_convert_fusion = bf16[512,2240]{0,1:T(8,128)(2,1)} fusion(bf16[512,2240]{0,1:T(8,128)(2,1)S(1)} %bitcast.74, bf16[2240,2240]{1,0:T(8,128)(2,1)} %all-gather.10.cloned.1.call-done), kind=kOutput, calls=%fused_computation.10 | convolution fusion | flops 5139169280 | bytes 14622720 | tf_op jit(solution)/shard_map/dot_general | solution.py:101
  475.5 4.8 reshape.38
  (38 shorter events, 11.4 us)
Async XLA Ops:
  6.5 104.7 %all-gather.8.cloned.1.call-start = ((), (), s32[]{:S(2)}) async-start(), calls=%async_computation | async-start | bytes 10035200 | tf_op jit(solution)/shard_map/all_gather | solution.py:85
  46.5 5.7 %copy-start.3 = (s32[2]{0:T(128)S(1)}, s32[2]{0:T(128)}, u32[]{:S(2)}) copy-start(s32[2]{0:T(128)} %param.13) | copy-start | bytes 28
  46.5 5.8 %copy-start.5 = (u32[32]{0:T(128)S(1)}, u32[32]{0:T(128)}, u32[]{:S(2)}) copy-start(u32[32]{0:T(128)} %constant.52) | copy-start | bytes 388
  46.5 9.5 %copy-start.4 = (s32[2]{0:T(128)S(1)}, s32[2]{0:T(128)}, u32[]{:S(2)}) copy-start(s32[2]{0:T(128)} %param.12) | copy-start | bytes 28
  52.1 150.9 %all-gather.14.cloned.1.call-start = ((), (), s32[]{:S(2)}) async-start(), calls=%async_computation.3 | async-start | bytes 5017600 | tf_op jit(solution)/shard_map/all_gather | solution.py:13
  125.0 13.2 %copy-start.1 = (bf16[2,2,128,2240]{2,3,1,0:T(8,128)(2,1)S(1)}, bf16[2,2,128,2240]{2,3,1,0:T(8,128)(2,1)}, u32[]{:S(2)}) copy-start(bf16[2,2,128,2240]{2,3,1,0:T(8,128)(2,1)} %param.9) | copy-start | bytes 6881284
  125.1 155.8 %all-gather.12.cloned.1.call-start = ((), (), s32[]{:S(2)}) async-start(), calls=%async_computation.2 | async-start | bytes 5017600 | tf_op jit(solution)/shard_map/all_gather | solution.py:13
  125.8 336.3 %all-gather.10.cloned.1.call-start = ((), (), s32[]{:S(2)}) async-start(), calls=%async_computation.1 | async-start | bytes 12902400 | tf_op jit(solution)/shard_map/all_gather | solution.py:103
  148.5 2.8 copy-start.2
  295.7 5.7 %copy-start = (bf16[2,256,20,112]{1,3,2,0:T(8,128)(2,1)S(1)}, bf16[2,256,20,112]{1,3,2,0:T(8,128)(2,1)}, u32[]{:S(2)}) copy-start(bf16[2,256,20,112]{1,3,2,0:T(8,128)(2,1)} %reshape.36) | copy-start | bytes 6881284
Sparse Core Ops, SparseCore 0:
  52.3 58.9 all-gather.7
  125.2 77.8 all-gather.13
  204.6 76.2 all-gather.11
  282.3 179.7 all-gather.9
